TPU v7x, 256 devices: a whole 4x4x8 slice. The times are simulated.
256 devices in a mesh: tm: 32 (over y_lo, z, core), gy: 8 (over y_hi, x).
Axes of the slice: x: 4, y: 4 (y_hi: 2, y_lo: 2; y = y_hi * 2 + y_lo), z: 8, core: 2. Of those that a mesh axis runs over, the one named last changes fastest.
Arguments:
- magnetic: bfloat16 [32, 3, 3, 1024, 1024], P('tm', None, None, 'gy'), may hold values from -6 to 6
- velocity: bfloat16 [32, 3, 1, 1024, 1024], P('tm', None, None, 'gy'), may hold values from -6 to 6
- mode_bin: int32 [1024, 1024], P(None, 'gy'), may hold values from 0 to 127, as said below
- omega_edges: int32 [9], replicated, may hold values from 0 to 32, as said below
Outputs:
- power: float32 [32, 1024, 1024], P('tm', None, 'gy')
- spectrum: float32 [8, 128], replicated
Inputs may be any that keep to these rules, and one draw needn't show every extreme that they name: mode_bin = 16 * p + q, where p is a level of min(kz, 1024 - kz) and q a level of min(ky, 1024 - ky); levels never fall as the wavenumber rises, and every value occurs. `omega_edges`: edges rise strictly, the first 0 and the last 32.
All inputs are finite; a program needn't handle non-finite values.
Results may differ from a plain program's by a relative error of at most 0.004.
The roundings to bfloat16 on the way count: a program that leaves them out, or rounds other values in their place, can miss the bound.
Values may be sent and summed in bfloat16 or wider, within the bound.
No kernel may reach another device: no remote copies, remote signals or barrier semaphores. Data moves between devices by JAX's collectives and lax.ppermute only.
A program may use at most 128 MiB of HBM per device.

v0:
```python
import math
import jax
import jax.numpy as jnp
from jax import lax
from jax.sharding import PartitionSpec as P

NBP = 8
NBQ = 16
NB_W = 8
hall_coef = 1.0
highest = lax.Precision.HIGHEST


def extended(cells, sides, width):
    for axis, dim in sides:
        count = lax.axis_size(axis)
        head = lax.slice_in_dim(cells, 0, width, axis=dim)
        tail = lax.slice_in_dim(cells, cells.shape[dim] - width, cells.shape[dim], axis=dim)
        cells = jnp.concatenate(
            [
                lax.ppermute(tail, axis, [(i, (i + 1) % count) for i in range(count)]),
                cells,
                lax.ppermute(head, axis, [((i + 1) % count, i) for i in range(count)]),
            ],
            axis=dim,
        )
    return cells


def window_taper_for(sample_moments, every_time_sample):
    return 0.5 - 0.5 * jnp.cos(
        2.0 * math.pi * (sample_moments.astype(jnp.float32) + 0.5) / every_time_sample
    )


def temporal_coefficients(angular_frequency, sample_moments, every_time_sample):
    phase_angles = jnp.mod(
        angular_frequency[:, None] * sample_moments[None, :], every_time_sample
    ).astype(jnp.float32)
    angles = 2.0 * math.pi * phase_angles / every_time_sample
    taper_weight = window_taper_for(sample_moments, every_time_sample)[None, :]
    return (
        (taper_weight * jnp.cos(angles)).astype(jnp.bfloat16),
        (-taper_weight * jnp.sin(angles)).astype(jnp.bfloat16),
    )


def dft_tables(length):
    series = jnp.arange(length, dtype=jnp.int32)
    phase_angles = jnp.mod(series[:, None] * series[None, :], length).astype(jnp.float32)
    angles = 2.0 * math.pi * phase_angles / length
    return (jnp.cos(angles).astype(jnp.bfloat16), jnp.sin(angles).astype(jnp.bfloat16))


def z_slope(values):
    return (jnp.roll(values, -1, axis=-1) - jnp.roll(values, 1, axis=-1)) * 0.5


def z_turn(re_part, im_part):
    zcos_tab, zsin_tab = dft_tables(re_part.shape[-1])
    turned_re = jnp.dot(re_part, zcos_tab, preferred_element_type=jnp.float32) + jnp.dot(
        im_part, zsin_tab, preferred_element_type=jnp.float32
    )
    turned_im = jnp.dot(im_part, zcos_tab, preferred_element_type=jnp.float32) - jnp.dot(
        re_part, zsin_tab, preferred_element_type=jnp.float32
    )
    return jnp.stack([turned_re, turned_im]).astype(jnp.bfloat16)


def electric_of(magnetic, velocity, slope_magz, slope_magx):
    inner = magnetic[:, :, 1:-1].astype(jnp.float32)
    x_slope = (
        magnetic[:, :, 2:].astype(jnp.float32) - magnetic[:, :, :-2].astype(jnp.float32)
    ) * 0.5
    mag_x, mag_y, mag_z = (inner[:, 0], inner[:, 1], inner[:, 2])
    cur_x = slope_magz - z_slope(mag_y)
    cur_y = z_slope(mag_x) - x_slope[:, 2]
    cur_z = x_slope[:, 1] - slope_magx
    flow = velocity.astype(jnp.float32)
    vel_x, vel_y, vel_z = (flow[:, 0], flow[:, 1], flow[:, 2])
    elec_x = -(vel_y * mag_z - vel_z * mag_y) + hall_coef * (cur_y * mag_z - cur_z * mag_y)
    elec_y = -(vel_z * mag_x - vel_x * mag_z) + hall_coef * (cur_z * mag_x - cur_x * mag_z)
    elec_z = -(vel_x * mag_y - vel_y * mag_x) + hall_coef * (cur_x * mag_y - cur_y * mag_x)
    return jnp.stack([elec_x, elec_y, elec_z], axis=1)


def body(magnetic, velocity, mode_bin, omega_edges):
    face_rows = jnp.stack([magnetic[:, 2, 1:-1], magnetic[:, 0, 1:-1]], axis=1)
    padded = extended(face_rows, (("gy", 3),), 1)
    slopes = (
        padded[:, :, :, 2:].astype(jnp.float32) - padded[:, :, :, :-2].astype(jnp.float32)
    ) * 0.5
    electric = electric_of(magnetic, velocity, slopes[:, 0], slopes[:, 1]).astype(jnp.bfloat16)
    local_t = electric.shape[0]
    z_count = electric.shape[-1]
    every_time_sample = local_t * lax.axis_size("tm")
    half_count = every_time_sample // 2
    owner_rank = lax.axis_index("tm")
    angular_frequency = owner_rank * local_t + jnp.arange(local_t, dtype=jnp.int32) - half_count
    time_segment = lax.all_gather(electric, "tm", axis=0, tiled=True)
    sample_moments = jnp.arange(time_segment.shape[0], dtype=jnp.int32)
    coefficient_real, coefficient_imaginary = temporal_coefficients(
        angular_frequency, sample_moments, every_time_sample
    )
    re_part = jnp.einsum(
        "wt,tcxyz->wcxyz", coefficient_real, time_segment, preferred_element_type=jnp.float32
    )
    im_part = jnp.einsum(
        "wt,tcxyz->wcxyz", coefficient_imaginary, time_segment, preferred_element_type=jnp.float32
    )
    moved = lax.all_to_all(
        z_turn(re_part.astype(jnp.bfloat16), im_part.astype(jnp.bfloat16)),
        "gy",
        split_axis=5,
        concat_axis=4,
        tiled=True,
    )
    y_count = moved.shape[4]
    ycos_tab, ysin_tab = dft_tables(y_count)
    wave_re = jnp.einsum(
        "wcxyk,yq->wcxqk", moved[0], ycos_tab, preferred_element_type=jnp.float32
    ) + jnp.einsum("wcxyk,yq->wcxqk", moved[1], ysin_tab, preferred_element_type=jnp.float32)
    wave_im = jnp.einsum(
        "wcxyk,yq->wcxqk", moved[1], ycos_tab, preferred_element_type=jnp.float32
    ) - jnp.einsum("wcxyk,yq->wcxqk", moved[0], ysin_tab, preferred_element_type=jnp.float32)
    power_map = jnp.sum(wave_re * wave_re + wave_im * wave_im, axis=(1, 2)) / (
        every_time_sample * y_count * z_count
    )
    kz_local = power_map.shape[2]
    block_rows = min(64, y_count)
    bin_total = NBP * NBQ
    bin_range = jnp.arange(bin_total, dtype=jnp.int32)

    def add_block(step_num, summed):
        row_block = lax.dynamic_slice_in_dim(
            power_map, step_num * block_rows, block_rows, 1
        ).reshape(local_t, block_rows * kz_local)
        bin_ids = lax.dynamic_slice_in_dim(mode_bin, step_num * block_rows, block_rows, 0).reshape(
            block_rows * kz_local
        )
        onehot = (bin_ids[:, None] == bin_range[None, :]).astype(jnp.float32)
        return summed + jnp.dot(row_block, onehot, precision=highest)

    by_mode = lax.fori_loop(
        0, y_count // block_rows, add_block, jnp.zeros((local_t, bin_total), jnp.float32)
    )
    omega = owner_rank * local_t + jnp.arange(local_t, dtype=jnp.int32)
    member = (
        (omega[None, :] >= omega_edges[:-1, None]) & (omega[None, :] < omega_edges[1:, None])
    ).astype(jnp.float32)
    partial_value = jnp.dot(member, by_mode, precision=highest)
    binned = lax.psum(partial_value, ("tm", "gy"))
    spectrum = jnp.log(
        binned * (NB_W * bin_total) / (every_time_sample * y_count * z_count) + 1e-06
    )
    return (power_map, spectrum)


def solution(mesh):
    return jax.shard_map(
        body,
        mesh=mesh,
        in_specs=(
            P("tm", None, None, "gy", None),
            P("tm", None, None, "gy", None),
            P(None, "gy"),
            P(),
        ),
        out_specs=(P("tm", None, "gy"), P()),
        check_vma=False,
    )
```

profile of v0, /device:TPU:1, one launch (start us, length us, event | category | flops | bytes accessed | tf_op | source)
XLA Modules:
  0.0 512.5 jit_solution(18000967554781323091)
XLA Ops:
  7.2 1.2 fusion.103
  8.5 6.0 %collective-permute-start = (bf16[1,2,1,1,1024]{4,3,2,1,0:T(2,128)(2,1)S(1)}, bf16[1,2,1,1,1024]{4,3,2,1,0:T(2,128)(2,1)S(1)}, u32[]{:S(2)}, u32[]{:S(2)}) collective-permute-start(bf16[1,2,1,1,1024]{4,3,2,1,0:T(2,128)(2,1)S(1)} %get-tuple-element.139), channel_id=1, source_target_pairs={{1,0},{2,1},{3,2},{4,3},{5,4},{6,5},{7,6},{0,7},{9,8},{10,9},{11,1... | collective-permute-start | bytes 12296 | tf_op jit(solution)/shard_map/ppermute | solution.py:23
  14.5 1.4 slice_convert_fusion
  16.7 3.9 collective-permute-done.1
  22.6 1.1 pad_maximum_fusion.1
  23.7 142.3 %all-gather.2.cloned.1.call-done = bf16[32,3,1,128,1024]{4,3,2,1,0:T(8,128)(2,1)} async-done(((bf16[1,3,1,128,1024]{4,3,2,1,0:T(8,128)(2,1)}), bf16[32,3,1,128,1024]{4,3,2,1,0:T(8,128)(2,1)}) %all-gather.2.cloned.1.call-update) | async-done | bytes 25165840 | tf_op jit(solution)/shard_map/all_gather | solution.py:100
  166.0 24.4 %fusion.5 = bf16[1,3,128,1024]{3,0,2,1:T(2,128)(2,1)S(1)} fusion(bf16[32,3,128,1024]{3,2,1,0:T(8,128)(2,1)} %bitcast.97, s32[]{:T(128)S(6)} %sub.139), kind=kOutput, calls=%fused_computation.8 | convolution fusion | flops 25166528 | bytes 25952260 | tf_op jit(solution)/shard_map/wt,tcxyz->wcxyz/dot_general | solution.py:108
  190.5 24.9 %fusion.7 = bf16[1,3,128,1024]{3,0,2,1:T(2,128)(2,1)S(1)} fusion(bf16[32,3,128,1024]{3,2,1,0:T(8,128)(2,1)} %bitcast.98, s32[]{:T(128)S(6)} %sub.139), kind=kOutput, calls=%fused_computation.10 | convolution fusion | flops 25166496 | bytes 25952260 | tf_op jit(solution)/shard_map/wt,tcxyz->wcxyz/dot_general | solution.py:105
  215.4 16.1 %fusion.21 = f32[3,128,1024]{2,1,0:T(8,128)S(1)} fusion(bf16[1,3,128,1024]{3,0,2,1:T(2,128)(2,1)S(1)} %fusion.7), kind=kOutput, calls=%fused_computation.27 | convolution fusion | flops 821035008 | bytes 2359296 | tf_op jit(solution)/shard_map/dot_general | solution.py:64
  231.5 16.1 %fusion.23 = f32[3,128,1024]{2,1,0:T(8,128)S(1)} fusion(bf16[1,3,128,1024]{3,0,2,1:T(2,128)(2,1)S(1)} %fusion.5), kind=kOutput, calls=%fused_computation.28 | convolution fusion | flops 821035008 | bytes 2359296 | tf_op jit(solution)/shard_map/dot_general | solution.py:61
  247.6 16.5 %fusion.42 = bf16[1,1,3,1,128,1024]{5,4,2,3,1,0:T(8,128)(2,1)S(1)} fusion(f32[3,128,1024]{2,1,0:T(8,128)S(1)} %fusion.21, bf16[1,3,128,1024]{3,0,2,1:T(2,128)(2,1)S(1)} %fusion.5), kind=kOutput, calls=%fused_computation.41 | convolution fusion | flops 821821440 | bytes 3145728 | tf_op jit(solution)/shard_map/dot_general | solution.py:64
  264.1 16.3 %fusion.39 = bf16[1,1,3,1,128,1024]{5,4,2,3,1,0:T(8,128)(2,1)S(1)} fusion(f32[3,128,1024]{2,1,0:T(8,128)S(1)} %fusion.23, bf16[1,3,128,1024]{3,0,2,1:T(2,128)(2,1)S(1)} %fusion.7), kind=kOutput, calls=%fused_computation.40 | convolution fusion | flops 821821440 | bytes 3145728 | tf_op jit(solution)/shard_map/dot_general | solution.py:61
  280.6 3.0 copy.44
  283.6 6.7 %all-to-all-start = ((bf16[2,1,3,1,128,1024]{4,0,3,2,1,5:T(2,128)(2,1)}), bf16[2,1,3,1,128,1024]{4,0,3,2,1,5:T(2,128)(2,1)S(1)}, u32[]{:S(2)}, u32[]{:S(2)}) async-start(bf16[2,1,3,1,128,1024]{4,0,3,2,1,5:T(2,128)(2,1)} %copy.44), calls=%async_computation | async-start | bytes 3145728 | tf_op jit(solution)/shard_map/all_to_all | solution.py:111
  290.4 22.9 %all-to-all-done = bf16[2,1,3,1,128,1024]{4,0,3,2,1,5:T(2,128)(2,1)S(1)} async-done(((bf16[2,1,3,1,128,1024]{4,0,3,2,1,5:T(2,128)(2,1)}), bf16[2,1,3,1,128,1024]{4,0,3,2,1,5:T(2,128)(2,1)S(1)}, u32[]{:S(2)}, u32[]{:S(2)}) %all-to-all-start) | async-done | bytes 1572896 | tf_op jit(solution)/shard_map/all_to_all | solution.py:111
  313.3 2.4 copy.45
  315.8 17.9 %fusion.29 = f32[1024,3,128]{2,0,1:T(8,128)S(1)} fusion(bf16[3,1024,128]{2,1,0:T(8,128)(2,1)S(1)} %bitcast.104), kind=kOutput, calls=%fused_computation.31 | convolution fusion | flops 821035008 | bytes 2359296 | tf_op jit(solution)/shard_map/wcxyk,yq->wcxqk/dot_general | solution.py:123
  333.7 18.0 %fusion.19 = f32[1024,3,128]{2,0,1:T(8,128)S(1)} fusion(bf16[3,1024,128]{2,1,0:T(8,128)(2,1)S(1)} %bitcast.105), kind=kOutput, calls=%fused_computation.26 | convolution fusion | flops 821035008 | bytes 2359296 | tf_op jit(solution)/shard_map/wcxyk,yq->wcxqk/dot_general | solution.py:122
  351.6 18.0 %fusion.17 = f32[1024,3,128]{2,0,1:T(8,128)S(1)} fusion(bf16[3,1024,128]{2,1,0:T(8,128)(2,1)S(1)} %bitcast.102), kind=kOutput, calls=%fused_computation.25 | convolution fusion | flops 821035008 | bytes 2359296 | tf_op jit(solution)/shard_map/wcxyk,yq->wcxqk/dot_general | solution.py:125
  369.6 18.0 %add_reduce_fusion = f32[1024,128]{1,0:T(8,128)S(1)} fusion(f32[1024,3,128]{2,0,1:T(8,128)S(1)} %fusion.29, f32[1024,3,128]{2,0,1:T(8,128)S(1)} %fusion.17, f32[1024,3,128]{2,0,1:T(8,128)S(1)} %fusion.19, bf16[3,1024,128]{2,1,0:T(8,128)(2,1)S(1)} %bitcast.103), kind=kOutput, calls=%fused_computation.36 | convolution fusion | flops 823263232 | bytes 6029312 | tf_op jit(solution)/shard_map/wcxyk,yq->wcxqk/dot_general | solution.py:120
  387.7 41.5 %while.14 = (s32[]{:T(128)}, f32[1,128]{1,0:T(1,128)S(1)}, f32[1,1024,128]{2,1,0:T(8,128)S(1)}, s32[1024,128]{1,0:T(8,128)}, s32[]{:T(128)}, /*index=5*/s32[]{:T(128)}, s32[]{:T(128)}, s32[]{:T(128)}) while((s32[]{:T(128)}, f32[1,128]{1,0:T(1,128)S(1)}, f32[1,1024,128]{2,1,0:T(8,128)S(1)}, s32[1024,128]{1,0:T(8,128)}, s32[]{:T(128)}, ...), condition=%wide.region_2.3_spmd.clone, body=%wide.region_1.2_spmd.clone.sunk | while | flops 13631751 | bytes 197789 | solution.py:144
  387.7 0.8 dynamic-slice_bitcast_fusion.2
  388.5 1.8 fusion.113
  390.3 0.8 dynamic-slice_bitcast_fusion.2
  391.1 1.8 fusion.113
  392.9 0.8 dynamic-slice_bitcast_fusion.2
  393.7 1.8 fusion.113
  395.5 0.8 dynamic-slice_bitcast_fusion.2
  396.3 1.8 fusion.113
  398.1 0.8 dynamic-slice_bitcast_fusion.2
  398.9 1.8 fusion.113
  400.7 0.8 dynamic-slice_bitcast_fusion.2
  401.5 1.8 fusion.113
  404.1 1.8 fusion.113
  405.9 0.8 dynamic-slice_bitcast_fusion.2
  406.6 1.8 fusion.113
  409.2 1.8 fusion.113
  411.8 1.8 fusion.113
  413.6 0.8 dynamic-slice_bitcast_fusion.2
  414.4 1.8 fusion.113
  417.0 1.8 fusion.113
  419.6 1.8 fusion.113
  421.4 0.8 dynamic-slice_bitcast_fusion.2
  422.2 1.8 fusion.113
  424.8 1.8 fusion.113
  426.6 0.8 dynamic-slice_bitcast_fusion.2
  427.4 1.8 fusion.113
  429.3 75.6 %psum.7 = f32[8,128]{1,0:T(8,128)S(1)} all-reduce(f32[8,128]{1,0:T(8,128)S(1)} %broadcast_multiply_fusion), channel_id=1, replica_groups=mesh['tm'=32,'gy'=8] {'tm','gy'}, use_global_device_ids=true, to_apply=%region_3.4 | all-reduce | flops 1024 | bytes 8192 | tf_op jit(solution)/shard_map/psum | solution.py:152
  (53 shorter events, 8.6 us)
Async XLA Ops:
  7.2 8.7 %copy-start = (bf16[1,3,3,128,1024]{4,3,2,1,0:T(8,128)(2,1)S(1)}, bf16[1,3,3,128,1024]{4,3,2,1,0:T(8,128)(2,1)}, u32[]{:S(2)}) copy-start(bf16[1,3,3,128,1024]{4,3,2,1,0:T(8,128)(2,1)} %param.6) | copy-start | bytes 7077892
  7.2 158.9 %all-gather.2.cloned.1.call-start = ((), (), s32[]{:S(2)}) async-start(), calls=%async_computation.1 | async-start | bytes 25952256 | tf_op jit(solution)/shard_map/all_gather | solution.py:100
  8.5 8.2 %collective-permute-start = (bf16[1,2,1,1,1024]{4,3,2,1,0:T(2,128)(2,1)S(1)}, bf16[1,2,1,1,1024]{4,3,2,1,0:T(2,128)(2,1)S(1)}, u32[]{:S(2)}, u32[]{:S(2)}) collective-permute-start(bf16[1,2,1,1,1024]{4,3,2,1,0:T(2,128)(2,1)S(1)} %get-tuple-element.139), channel_id=1, source_target_pairs={{1,0},{2,1},{3,2},{4,3},{5,4},{6,5},{7,6},{0,7},{9,8},{10,9},{11,1... | collective-permute-start | bytes 12296 | tf_op jit(solution)/shard_map/ppermute | solution.py:23
  14.5 2.0 copy-start.2
  14.5 6.1 %collective-permute-start.1 = (bf16[1,2,1,1,1024]{4,3,2,1,0:T(2,128)(2,1)S(1)}, bf16[1,2,1,1,1024]{4,3,2,1,0:T(2,128)(2,1)S(1)}, u32[]{:S(2)}, u32[]{:S(2)}) collective-permute-start(bf16[1,2,1,1,1024]{4,3,2,1,0:T(2,128)(2,1)S(1)} %get-tuple-element.140), channel_id=1, source_target_pairs={{0,1},{1,2},{2,3},{3,4},{4,5},{5,6},{6,7},{7,0},{8,9},{9,10},{10,1... | collective-permute-start | bytes 12296 | tf_op jit(solution)/shard_map/ppermute | solution.py:21
  280.4 9.9 %copy-start.3 = (s32[9]{0:T(128)S(1)}, s32[9]{0:T(128)}, u32[]{:S(2)}) copy-start(s32[9]{0:T(128)} %param.9) | copy-start | bytes 112
  283.6 29.7 %all-to-all-start = ((bf16[2,1,3,1,128,1024]{4,0,3,2,1,5:T(2,128)(2,1)}), bf16[2,1,3,1,128,1024]{4,0,3,2,1,5:T(2,128)(2,1)S(1)}, u32[]{:S(2)}, u32[]{:S(2)}) async-start(bf16[2,1,3,1,128,1024]{4,0,3,2,1,5:T(2,128)(2,1)} %copy.44), calls=%async_computation | async-start | bytes 3145728 | tf_op jit(solution)/shard_map/all_to_all | solution.py:111
  429.2 76.3 %copy-start.1 = (f32[1,1024,128]{2,1,0:T(8,128)}, f32[1,1024,128]{2,1,0:T(8,128)S(1)}, u32[]{:S(2)}) copy-start(f32[1,1024,128]{2,1,0:T(8,128)S(1)} %get-tuple-element.195) | copy-start | bytes 1572868
Sparse Core Ops, SparseCore 0:
  23.8 142.1 all-gather.1
where the time goes:
time: 518 us; the launch traced here: 513 us
  matrix products  215 us (42%)
  waiting for transfers between devices  169 us (33%)
  blocking collectives  75.6 us (15%)
  local copies, waits for them, and re-layouts  19.7 us (4%)
  between operations  14.5 us (3%)
  starting transfers between devices  12.7 us (2%)
  other arithmetic  5.55 us (1%)
    all_gather x1, waiting for transfers between devices, body(): time_segment = lax.all_gather(electric, 'tm', axis=0, tiled=True)  142 us
    psum x1, blocking collectives, body(): binned = lax.psum(partial_value, ('tm', 'gy'))  75.6 us
    dot_general x16, matrix products, add_block(): return summed + jnp.dot(row_block, onehot, precision=highest)  28.7 us
    dot_general x1, matrix products, body(): jnp.einsum('wt,tcxyz->wcxyz', coefficient_real, time_segment, preferred_e...  24.9 us
    dot_general x1, matrix products, body(): jnp.einsum('wt,tcxyz->wcxyz', coefficient_imaginary, time_segment, prefer...  24.4 us
    all_to_all x1, waiting for transfers between devices, body(): lax.all_to_all(z_turn(re_part.astype(jnp.bfloat16), im_part.astype(jnp.bf...  22.9 us
    dot_general x1, matrix products, body(): jnp.einsum('wcxyk,yq->wcxqk', moved[0], ycos_tab, preferred_element_type=...  18 us
    dot_general x1, matrix products, body(): jnp.einsum('wcxyk,yq->wcxqk', moved[1], ysin_tab, preferred_element_type=...  18 us
  transfers between devices with their start and end apart: 4, of which 3 were waited for; matrix products, arithmetic and copies ran while one was open for 0% of the time, Pallas kernels for 0%

commit v1 on v0

--- a/solution.py
+++ b/solution.py
@@ -9,6 +9,12 @@
 NB_W = 8
 hall_coef = 1.0
 highest = lax.Precision.HIGHEST
+
+
+def name_pairs_all_here(local_x):
+    for j in ("gy", "tm"):
+        local_x = jax.lax.psum(local_x, axis_name=j)
+    return local_x
 
 
 def extended(cells, sides, width):
@@ -149,7 +155,7 @@
         (omega[None, :] >= omega_edges[:-1, None]) & (omega[None, :] < omega_edges[1:, None])
     ).astype(jnp.float32)
     partial_value = jnp.dot(member, by_mode, precision=highest)
-    binned = lax.psum(partial_value, ("tm", "gy"))
+    binned = name_pairs_all_here(partial_value)
     spectrum = jnp.log(
         binned * (NB_W * bin_total) / (every_time_sample * y_count * z_count) + 1e-06
     )

time: 518 us -> 517 us (level)
    psum x1 -> x2, blocking collectives: 75.6 us -> 75.1 us  [name_pairs_all_here(): local_x = jax.lax.psum(local_x, axis_name=j)]
where the time goes in v1:
time: 517 us; the launch traced here: 512 us
  matrix products  215 us (42%)
  waiting for transfers between devices  169 us (33%)
  blocking collectives  75.1 us (15%)
  local copies, waits for them, and re-layouts  19.6 us (4%)
  between operations  14.5 us (3%)
  starting transfers between devices  12.7 us (2%)
  other arithmetic  5.53 us (1%)
    all_gather x1, waiting for transfers between devices, body(): time_segment = lax.all_gather(electric, 'tm', axis=0, tiled=True)  142 us
    psum x2, blocking collectives, name_pairs_all_here(): local_x = jax.lax.psum(local_x, axis_name=j)  75.1 us
    dot_general x16, matrix products, add_block(): return summed + jnp.dot(row_block, onehot, precision=highest)  28.7 us
    dot_general x1, matrix products, body(): jnp.einsum('wt,tcxyz->wcxyz', coefficient_real, time_segment, preferred_e...  24.9 us
    dot_general x1, matrix products, body(): jnp.einsum('wt,tcxyz->wcxyz', coefficient_imaginary, time_segment, prefer...  24.4 us
    all_to_all x1, waiting for transfers between devices, body(): lax.all_to_all(z_turn(re_part.astype(jnp.bfloat16), im_part.astype(jnp.bf...  22.9 us
    dot_general x1, matrix products, body(): jnp.einsum('wcxyk,yq->wcxqk', moved[0], ycos_tab, preferred_element_type=...  18 us
    dot_general x1, matrix products, body(): jnp.einsum('wcxyk,yq->wcxqk', moved[1], ysin_tab, preferred_element_type=...  18 us
  transfers between devices with their start and end apart: 4, of which 3 were waited for; matrix products, arithmetic and copies ran while one was open for 0% of the time, Pallas kernels for 0%

profile of v1, /device:TPU:1, one launch (start us, length us, event | category | flops | bytes accessed | tf_op | source)
XLA Modules:
  0.0 511.9 jit_solution(6100909402852429790)
XLA Ops:
  7.2 1.2 fusion.103
  8.5 6.0 %collective-permute-start = (bf16[1,2,1,1,1024]{4,3,2,1,0:T(2,128)(2,1)S(1)}, bf16[1,2,1,1,1024]{4,3,2,1,0:T(2,128)(2,1)S(1)}, u32[]{:S(2)}, u32[]{:S(2)}) collective-permute-start(bf16[1,2,1,1,1024]{4,3,2,1,0:T(2,128)(2,1)S(1)} %get-tuple-element.139), channel_id=1, source_target_pairs={{1,0},{2,1},{3,2},{4,3},{5,4},{6,5},{7,6},{0,7},{9,8},{10,9},{11,1... | collective-permute-start | bytes 12296 | tf_op jit(solution)/shard_map/ppermute | solution.py:29
  14.5 1.4 slice_convert_fusion
  16.7 3.9 collective-permute-done.1
  22.6 1.0 pad_maximum_fusion.1
  23.7 142.3 %all-gather.2.cloned.1.call-done = bf16[32,3,1,128,1024]{4,3,2,1,0:T(8,128)(2,1)} async-done(((bf16[1,3,1,128,1024]{4,3,2,1,0:T(8,128)(2,1)}), bf16[32,3,1,128,1024]{4,3,2,1,0:T(8,128)(2,1)}) %all-gather.2.cloned.1.call-update) | async-done | bytes 25165840 | tf_op jit(solution)/shard_map/all_gather | solution.py:106
  166.0 24.4 %fusion.5 = bf16[1,3,128,1024]{3,0,2,1:T(2,128)(2,1)S(1)} fusion(bf16[32,3,128,1024]{3,2,1,0:T(8,128)(2,1)} %bitcast.97, s32[]{:T(128)S(6)} %sub.139), kind=kOutput, calls=%fused_computation.8 | convolution fusion | flops 25166528 | bytes 25952260 | tf_op jit(solution)/shard_map/wt,tcxyz->wcxyz/dot_general | solution.py:114
  190.5 24.9 %fusion.7 = bf16[1,3,128,1024]{3,0,2,1:T(2,128)(2,1)S(1)} fusion(bf16[32,3,128,1024]{3,2,1,0:T(8,128)(2,1)} %bitcast.98, s32[]{:T(128)S(6)} %sub.139), kind=kOutput, calls=%fused_computation.10 | convolution fusion | flops 25166496 | bytes 25952260 | tf_op jit(solution)/shard_map/wt,tcxyz->wcxyz/dot_general | solution.py:111
  215.4 16.1 %fusion.21 = f32[3,128,1024]{2,1,0:T(8,128)S(1)} fusion(bf16[1,3,128,1024]{3,0,2,1:T(2,128)(2,1)S(1)} %fusion.7), kind=kOutput, calls=%fused_computation.27 | convolution fusion | flops 821035008 | bytes 2359296 | tf_op jit(solution)/shard_map/dot_general | solution.py:70
  231.5 16.1 %fusion.23 = f32[3,128,1024]{2,1,0:T(8,128)S(1)} fusion(bf16[1,3,128,1024]{3,0,2,1:T(2,128)(2,1)S(1)} %fusion.5), kind=kOutput, calls=%fused_computation.28 | convolution fusion | flops 821035008 | bytes 2359296 | tf_op jit(solution)/shard_map/dot_general | solution.py:67
  247.6 16.5 %fusion.42 = bf16[1,1,3,1,128,1024]{5,4,2,3,1,0:T(8,128)(2,1)S(1)} fusion(f32[3,128,1024]{2,1,0:T(8,128)S(1)} %fusion.21, bf16[1,3,128,1024]{3,0,2,1:T(2,128)(2,1)S(1)} %fusion.5), kind=kOutput, calls=%fused_computation.41 | convolution fusion | flops 821821440 | bytes 3145728 | tf_op jit(solution)/shard_map/dot_general | solution.py:70
  264.1 16.3 %fusion.39 = bf16[1,1,3,1,128,1024]{5,4,2,3,1,0:T(8,128)(2,1)S(1)} fusion(f32[3,128,1024]{2,1,0:T(8,128)S(1)} %fusion.23, bf16[1,3,128,1024]{3,0,2,1:T(2,128)(2,1)S(1)} %fusion.7), kind=kOutput, calls=%fused_computation.40 | convolution fusion | flops 821821440 | bytes 3145728 | tf_op jit(solution)/shard_map/dot_general | solution.py:67
  280.6 3.0 copy.44
  283.6 6.7 %all-to-all-start = ((bf16[2,1,3,1,128,1024]{4,0,3,2,1,5:T(2,128)(2,1)}), bf16[2,1,3,1,128,1024]{4,0,3,2,1,5:T(2,128)(2,1)S(1)}, u32[]{:S(2)}, u32[]{:S(2)}) async-start(bf16[2,1,3,1,128,1024]{4,0,3,2,1,5:T(2,128)(2,1)} %copy.44), calls=%async_computation | async-start | bytes 3145728 | tf_op jit(solution)/shard_map/all_to_all | solution.py:117
  290.3 22.9 %all-to-all-done = bf16[2,1,3,1,128,1024]{4,0,3,2,1,5:T(2,128)(2,1)S(1)} async-done(((bf16[2,1,3,1,128,1024]{4,0,3,2,1,5:T(2,128)(2,1)}), bf16[2,1,3,1,128,1024]{4,0,3,2,1,5:T(2,128)(2,1)S(1)}, u32[]{:S(2)}, u32[]{:S(2)}) %all-to-all-start) | async-done | bytes 1572896 | tf_op jit(solution)/shard_map/all_to_all | solution.py:117
  313.2 2.4 copy.45
  315.7 17.9 %fusion.29 = f32[1024,3,128]{2,0,1:T(8,128)S(1)} fusion(bf16[3,1024,128]{2,1,0:T(8,128)(2,1)S(1)} %bitcast.104), kind=kOutput, calls=%fused_computation.31 | convolution fusion | flops 821035008 | bytes 2359296 | tf_op jit(solution)/shard_map/wcxyk,yq->wcxqk/dot_general | solution.py:129
  333.6 18.0 %fusion.19 = f32[1024,3,128]{2,0,1:T(8,128)S(1)} fusion(bf16[3,1024,128]{2,1,0:T(8,128)(2,1)S(1)} %bitcast.105), kind=kOutput, calls=%fused_computation.26 | convolution fusion | flops 821035008 | bytes 2359296 | tf_op jit(solution)/shard_map/wcxyk,yq->wcxqk/dot_general | solution.py:128
  351.6 18.0 %fusion.17 = f32[1024,3,128]{2,0,1:T(8,128)S(1)} fusion(bf16[3,1024,128]{2,1,0:T(8,128)(2,1)S(1)} %bitcast.102), kind=kOutput, calls=%fused_computation.25 | convolution fusion | flops 821035008 | bytes 2359296 | tf_op jit(solution)/shard_map/wcxyk,yq->wcxqk/dot_general | solution.py:131
  369.5 18.0 %add_reduce_fusion = f32[1024,128]{1,0:T(8,128)S(1)} fusion(f32[1024,3,128]{2,0,1:T(8,128)S(1)} %fusion.29, f32[1024,3,128]{2,0,1:T(8,128)S(1)} %fusion.17, f32[1024,3,128]{2,0,1:T(8,128)S(1)} %fusion.19, bf16[3,1024,128]{2,1,0:T(8,128)(2,1)S(1)} %bitcast.103), kind=kOutput, calls=%fused_computation.36 | convolution fusion | flops 823263232 | bytes 6029312 | tf_op jit(solution)/shard_map/wcxyk,yq->wcxqk/dot_general | solution.py:126
  387.6 41.5 %while.14 = (s32[]{:T(128)}, f32[1,128]{1,0:T(1,128)S(1)}, f32[1,1024,128]{2,1,0:T(8,128)S(1)}, s32[1024,128]{1,0:T(8,128)}, s32[]{:T(128)}, /*index=5*/s32[]{:T(128)}, s32[]{:T(128)}, s32[]{:T(128)}) while((s32[]{:T(128)}, f32[1,128]{1,0:T(1,128)S(1)}, f32[1,1024,128]{2,1,0:T(8,128)S(1)}, s32[1024,128]{1,0:T(8,128)}, s32[]{:T(128)}, ...), condition=%wide.region_2.3_spmd.clone, body=%wide.region_1.2_spmd.clone.sunk | while | flops 13631751 | bytes 197789 | solution.py:150
  387.7 0.8 dynamic-slice_bitcast_fusion.2
  388.4 1.8 fusion.113
  390.2 0.8 dynamic-slice_bitcast_fusion.2
  391.0 1.8 fusion.113
  393.6 1.8 fusion.113
  396.2 1.8 fusion.113
  398.0 0.8 dynamic-slice_bitcast_fusion.2
  398.8 1.8 fusion.113
  401.4 1.8 fusion.113
  403.2 0.8 dynamic-slice_bitcast_fusion.2
  404.0 1.8 fusion.113
  405.8 0.8 dynamic-slice_bitcast_fusion.2
  406.6 1.8 fusion.113
  409.2 1.8 fusion.113
  411.0 0.8 dynamic-slice_bitcast_fusion.2
  411.7 1.8 fusion.113
  414.3 1.8 fusion.113
  416.9 1.8 fusion.113
  418.7 0.8 dynamic-slice_bitcast_fusion.2
  419.5 1.8 fusion.113
  422.1 1.8 fusion.113
  423.9 0.8 dynamic-slice_bitcast_fusion.2
  424.7 1.8 fusion.113
  426.5 0.8 dynamic-slice_bitcast_fusion.2
  427.3 1.8 fusion.113
  429.2 17.7 %psum.14 = f32[8,128]{1,0:T(8,128)S(1)} all-reduce(f32[8,128]{1,0:T(8,128)S(1)} %broadcast_multiply_fusion), channel_id=1, replica_groups=mesh['tm'=32,'gy'=8] {'gy'}, use_global_device_ids=true, to_apply=%region_3.4 | all-reduce | flops 1024 | bytes 8192 | tf_op jit(solution)/shard_map/psum | solution.py:16
  446.9 57.3 %psum.15 = f32[8,128]{1,0:T(8,128)S(1)} all-reduce(f32[8,128]{1,0:T(8,128)S(1)} %psum.14), channel_id=1, replica_groups=mesh['tm'=32,'gy'=8] {'tm'}, use_global_device_ids=true, to_apply=%region_4.5 | all-reduce | flops 1024 | bytes 8192 | tf_op jit(solution)/shard_map/psum | solution.py:16
  (54 shorter events, 9.3 us)
Async XLA Ops:
  7.2 8.7 %copy-start = (bf16[1,3,3,128,1024]{4,3,2,1,0:T(8,128)(2,1)S(1)}, bf16[1,3,3,128,1024]{4,3,2,1,0:T(8,128)(2,1)}, u32[]{:S(2)}) copy-start(bf16[1,3,3,128,1024]{4,3,2,1,0:T(8,128)(2,1)} %param.6) | copy-start | bytes 7077892
  7.2 158.9 %all-gather.2.cloned.1.call-start = ((), (), s32[]{:S(2)}) async-start(), calls=%async_computation.1 | async-start | bytes 25952256 | tf_op jit(solution)/shard_map/all_gather | solution.py:106
  8.5 8.2 %collective-permute-start = (bf16[1,2,1,1,1024]{4,3,2,1,0:T(2,128)(2,1)S(1)}, bf16[1,2,1,1,1024]{4,3,2,1,0:T(2,128)(2,1)S(1)}, u32[]{:S(2)}, u32[]{:S(2)}) collective-permute-start(bf16[1,2,1,1,1024]{4,3,2,1,0:T(2,128)(2,1)S(1)} %get-tuple-element.139), channel_id=1, source_target_pairs={{1,0},{2,1},{3,2},{4,3},{5,4},{6,5},{7,6},{0,7},{9,8},{10,9},{11,1... | collective-permute-start | bytes 12296 | tf_op jit(solution)/shard_map/ppermute | solution.py:29
  14.5 2.0 copy-start.2
  14.5 6.1 %collective-permute-start.1 = (bf16[1,2,1,1,1024]{4,3,2,1,0:T(2,128)(2,1)S(1)}, bf16[1,2,1,1,1024]{4,3,2,1,0:T(2,128)(2,1)S(1)}, u32[]{:S(2)}, u32[]{:S(2)}) collective-permute-start(bf16[1,2,1,1,1024]{4,3,2,1,0:T(2,128)(2,1)S(1)} %get-tuple-element.140), channel_id=1, source_target_pairs={{0,1},{1,2},{2,3},{3,4},{4,5},{5,6},{6,7},{7,0},{8,9},{9,10},{10,1... | collective-permute-start | bytes 12296 | tf_op jit(solution)/shard_map/ppermute | solution.py:27
  280.4 9.8 %copy-start.3 = (s32[9]{0:T(128)S(1)}, s32[9]{0:T(128)}, u32[]{:S(2)}) copy-start(s32[9]{0:T(128)} %param.9) | copy-start | bytes 112
  283.6 29.6 %all-to-all-start = ((bf16[2,1,3,1,128,1024]{4,0,3,2,1,5:T(2,128)(2,1)}), bf16[2,1,3,1,128,1024]{4,0,3,2,1,5:T(2,128)(2,1)S(1)}, u32[]{:S(2)}, u32[]{:S(2)}) async-start(bf16[2,1,3,1,128,1024]{4,0,3,2,1,5:T(2,128)(2,1)} %copy.44), calls=%async_computation | async-start | bytes 3145728 | tf_op jit(solution)/shard_map/all_to_all | solution.py:117
  429.1 75.7 %copy-start.1 = (f32[1,1024,128]{2,1,0:T(8,128)}, f32[1,1024,128]{2,1,0:T(8,128)S(1)}, u32[]{:S(2)}) copy-start(f32[1,1024,128]{2,1,0:T(8,128)S(1)} %get-tuple-element.195) | copy-start | bytes 1572868
Sparse Core Ops, SparseCore 0:
  23.8 142.1 all-gather.1
